TPU v7x, 32 devices: a whole 2x2x4 slice. The times are simulated.
32 devices in a mesh: energy: 8 (over y, x, core), cuts: 4 (over z).
Axes of the slice: x: 2, y: 2, z: 4, core: 2. Of those that a mesh axis runs over, the one named last changes fastest.
Arguments:
- green_diag: bfloat16 [4, 32, 2, 256, 256], P('cuts', 'energy'), may hold values from -0.375 to 0.375
- green_upper: bfloat16 [4, 32, 2, 256, 256], P('cuts', 'energy'), may hold values from -0.375 to 0.375
- sigma_lesser: bfloat16 [4, 32, 2, 256, 256], P('cuts', 'energy'), may hold values from -6 to 6
- screening: bfloat16 [4, 32, 2, 256, 256], P('cuts', 'energy'), may hold values from -0.375 to 0.375
Outputs:
- polar_screened: bfloat16 [4, 32, 2, 256, 256], P('cuts', 'energy')
All inputs are finite; a program needn't handle non-finite values.
Results may differ from a plain program's by a relative error of at most 0.013.
Values may be sent and summed in bfloat16 or wider, within the bound.
A program may use at most 64 MiB of HBM per device.

v0:
```python
import math
import jax
import jax.numpy as jnp
from jax import lax
from jax.sharding import PartitionSpec as P


def shifted(value, axis, steps):
    count = lax.axis_size(axis)
    leading, last = (max(0, -steps), min(count, count - steps))
    return lax.ppermute(value, axis, [(source, source + steps) for source in range(leading, last)])


def times_block(left, right):
    real = jnp.einsum(
        "eij,ejk->eik", left[:, 0], right[:, 0], preferred_element_type=jnp.float32
    ) - jnp.einsum("eij,ejk->eik", left[:, 1], right[:, 1], preferred_element_type=jnp.float32)
    imag = jnp.einsum(
        "eij,ejk->eik", left[:, 0], right[:, 1], preferred_element_type=jnp.float32
    ) + jnp.einsum("eij,ejk->eik", left[:, 1], right[:, 0], preferred_element_type=jnp.float32)
    return jnp.stack([real, imag], axis=1)


def times_adjoint(left, right):
    real = jnp.einsum(
        "eij,ekj->eik", left[:, 0], right[:, 0], preferred_element_type=jnp.float32
    ) + jnp.einsum("eij,ekj->eik", left[:, 1], right[:, 1], preferred_element_type=jnp.float32)
    imag = jnp.einsum(
        "eij,ekj->eik", left[:, 1], right[:, 0], preferred_element_type=jnp.float32
    ) - jnp.einsum("eij,ekj->eik", left[:, 0], right[:, 1], preferred_element_type=jnp.float32)
    return jnp.stack([real, imag], axis=1)


def angle_table(rows_count, cols_count, period):
    row_index = lax.broadcasted_iota(jnp.int32, (rows_count, cols_count), 0)
    col_index = lax.broadcasted_iota(jnp.int32, (rows_count, cols_count), 1)
    phase = (row_index * col_index % period).astype(jnp.float32)
    return phase * (2.0 * math.pi / period)


def split_table_dot(table, data):
    upper = table.astype(jnp.bfloat16)
    lower = (table - upper.astype(jnp.float32)).astype(jnp.bfloat16)
    return jnp.dot(upper, data, preferred_element_type=jnp.float32) + jnp.dot(
        lower, data, preferred_element_type=jnp.float32
    )


def correlate(spread):
    energies = spread.shape[0]
    period = 2 * energies
    forward = angle_table(period, energies, period)
    inverse = angle_table(energies, period, period)
    cos_inv = jnp.cos(inverse)
    sin_inv = jnp.sin(inverse)
    high = lax.Precision.HIGHEST
    real_part = spread[:, 0].reshape(energies, -1)
    imag_part = spread[:, 1].reshape(energies, -1)
    width = real_part.shape[1]
    joined = jnp.concatenate([real_part, imag_part], axis=1)
    cos_both = split_table_dot(jnp.cos(forward), joined)
    sin_both = split_table_dot(jnp.sin(forward), joined)
    spec_real = cos_both[:, :width] + sin_both[:, width:]
    spec_imag = cos_both[:, width:] - sin_both[:, :width]
    power = spec_real * spec_real + spec_imag * spec_imag
    lag_real = jnp.dot(cos_inv, power, precision=high) / period
    lag_imag = jnp.dot(sin_inv, power, precision=high) / period
    polar = jnp.stack([lag_real, lag_imag], axis=1) / energies
    return polar.reshape(spread.shape).astype(jnp.bfloat16)


def shards(green_diag, green_upper, sigma_lesser, screening):
    sigma_next = shifted(sigma_lesser, "cuts", -1)
    own_term = times_block(green_diag[0], sigma_lesser[0]).astype(jnp.bfloat16)
    pair_term = times_block(green_upper[0], sigma_next[0]).astype(jnp.bfloat16)
    lesser = (
        times_adjoint(own_term, green_diag[0]) + times_adjoint(pair_term, green_upper[0])
    ).astype(jnp.bfloat16)
    entries = lax.all_to_all(lesser, "energy", split_axis=2, concat_axis=0, tiled=True)
    polar_rows = correlate(entries)
    back_field = lax.all_to_all(polar_rows, "energy", split_axis=0, concat_axis=2, tiled=True)
    screened_left = times_block(screening[0], back_field).astype(jnp.bfloat16)
    result_field = times_adjoint(screened_left, screening[0]).astype(jnp.bfloat16)
    return result_field[None]


def solution(mesh):
    in_specs = (
        P("cuts", "energy", None, None, None),
        P("cuts", "energy", None, None, None),
        P("cuts", "energy", None, None, None),
        P("cuts", "energy", None, None, None),
    )
    out_specs = P("cuts", "energy", None, None, None)
    return jax.shard_map(shards, mesh=mesh, in_specs=in_specs, out_specs=out_specs, check_vma=False)
```

profile of v0, /device:TPU:0, one launch (start us, length us, event | category | flops | bytes accessed | tf_op | source)
XLA Modules:
  0.0 84.3 jit_solution(1953093069969859186)
XLA Ops:
  0.0 1.4 %copy.97 = bf16[1,4,2,256,256]{4,3,1,2,0:T(8,128)(2,1)S(1)} copy(bf16[1,4,2,256,256]{4,3,2,1,0:T(8,128)(2,1)} %param.6) | data formatting | bytes 2097152 | tf_op args[2]
  1.4 1.3 %collective-permute-start = (bf16[1,4,2,256,256]{4,3,1,2,0:T(8,128)(2,1)S(1)}, bf16[1,4,2,256,256]{4,3,1,2,0:T(8,128)(2,1)S(1)}, u32[]{:S(2)}, u32[]{:S(2)}) collective-permute-start(bf16[1,4,2,256,256]{4,3,1,2,0:T(8,128)(2,1)S(1)} %copy.97), channel_id=1, source_target_pairs={{1,0},{2,1},{3,2},{5,4},{6,5},{7,6},{9,8},{10,9},{11,10},{13,12},{... | collective-permute-start | bytes 3145736 | tf_op jit(solution)/shard_map/ppermute | solution.py:11
  4.0 0.6 copy-done.1
  6.0 23.5 %collective-permute-done = bf16[1,4,2,256,256]{4,3,1,2,0:T(8,128)(2,1)S(1)} collective-permute-done((bf16[1,4,2,256,256]{4,3,1,2,0:T(8,128)(2,1)S(1)}, bf16[1,4,2,256,256]{4,3,1,2,0:T(8,128)(2,1)S(1)}, u32[]{:S(2)}, u32[]{:S(2)}) %collective-permute-start) | collective-permute-done | bytes 1048608 | tf_op jit(solution)/shard_map/ppermute | solution.py:11
  32.1 0.4 fusion.3
  32.5 0.8 copy.65
  33.3 19.0 %all_to_all.36 = bf16[4,2,256,256]{3,0,1,2:T(4,128)(2,1)S(1)} all-to-all(bf16[4,2,256,256]{3,0,1,2:T(4,128)(2,1)S(1)} %copy.65), channel_id=1, replica_groups=mesh['energy'=8,'cuts'=4] {'energy'}, dimensions={2} | all-to-all | bytes 2097152 | tf_op jit(solution)/shard_map/all_to_all | solution.py:79
  53.4 0.8 fusion.51
  54.2 0.8 fusion.48
  55.0 0.8 convolution_add_fusion.1
  55.9 0.8 convolution_add_fusion
  56.7 0.4 fusion.1
  57.1 1.2 %convolution_multiply_fusion.1 = f32[32,8192]{1,0:T(8,128)S(1)} fusion(f32[64,8192]{1,0:T(8,128)S(1)} %fusion.1), kind=kOutput, calls=%fused_computation.3 | convolution fusion | flops 201617408 | bytes 3145728 | tf_op jit(solution)/shard_map/dot_general | solution.py:66
  58.3 1.2 %convolution_multiply_fusion = f32[32,8192]{1,0:T(8,128)S(1)} fusion(f32[64,8192]{1,0:T(8,128)S(1)} %fusion.1), kind=kOutput, calls=%fused_computation.2 | convolution fusion | flops 201617408 | bytes 3145728 | tf_op jit(solution)/shard_map/dot_general | solution.py:67
  60.1 1.3 %fusion.4 = bf16[32,2,32,256]{3,2,1,0:T(8,128)(2,1)} fusion(f32[32,1,32,256]{3,2,1,0:T(8,128)S(1)} %bitcast.167, f32[32,1,32,256]{3,2,1,0:T(8,128)S(1)} %bitcast.165), kind=kLoop, calls=%fused_computation.12 | loop fusion | flops 1572864 | bytes 3145728 | tf_op jit(solution)/shard_map/convert_element_type | solution.py:69
  61.4 3.6 %all-to-all-start.1 = ((bf16[32,2,32,256]{3,2,1,0:T(8,128)(2,1)}), bf16[32,2,32,256]{3,2,1,0:T(8,128)(2,1)S(1)}, u32[]{:S(2)}, u32[]{:S(2)}) async-start(bf16[32,2,32,256]{3,2,1,0:T(8,128)(2,1)} %fusion.4), calls=%async_computation.1 | async-start | bytes 2097152 | tf_op jit(solution)/shard_map/all_to_all | solution.py:81
  65.1 15.2 %all-to-all-done.1 = bf16[32,2,32,256]{3,2,1,0:T(8,128)(2,1)S(1)} async-done(((bf16[32,2,32,256]{3,2,1,0:T(8,128)(2,1)}), bf16[32,2,32,256]{3,2,1,0:T(8,128)(2,1)S(1)}, u32[]{:S(2)}, u32[]{:S(2)}) %all-to-all-start.1) | async-done | bytes 1048608 | tf_op jit(solution)/shard_map/all_to_all | solution.py:81
  80.7 0.3 fusion.24
  81.1 0.3 fusion.13
  81.8 0.3 fusion.14
  82.1 0.3 fusion.29
  82.5 0.4 fusion.18
  82.8 0.3 fusion.17
  83.3 1.0 %copy.78 = bf16[1,4,2,256,256]{4,3,2,1,0:T(8,128)(2,1)} copy(bf16[1,4,2,256,256]{4,3,1,2,0:T(8,128)(2,1)S(1)} %pad_maximum_fusion) | data formatting | bytes 2097152 | tf_op jit(solution)/shard_map/stack | solution.py:31
  (37 shorter events, 7.8 us)
Async XLA Ops:
  0.0 2.7 %copy-start = (bf16[1,4,2,256,256]{4,3,2,1,0:T(8,128)(2,1)S(1)}, bf16[1,4,2,256,256]{4,3,2,1,0:T(8,128)(2,1)}, u32[]{:S(2)}) copy-start(bf16[1,4,2,256,256]{4,3,2,1,0:T(8,128)(2,1)} %param.4) | copy-start | bytes 3145732
  1.4 28.1 %collective-permute-start = (bf16[1,4,2,256,256]{4,3,1,2,0:T(8,128)(2,1)S(1)}, bf16[1,4,2,256,256]{4,3,1,2,0:T(8,128)(2,1)S(1)}, u32[]{:S(2)}, u32[]{:S(2)}) collective-permute-start(bf16[1,4,2,256,256]{4,3,1,2,0:T(8,128)(2,1)S(1)} %copy.97), channel_id=1, source_target_pairs={{1,0},{2,1},{3,2},{5,4},{6,5},{7,6},{9,8},{10,9},{11,10},{13,12},{... | collective-permute-start | bytes 3145736 | tf_op jit(solution)/shard_map/ppermute | solution.py:11
  3.4 1.2 %copy-start.1 = (bf16[1,4,2,256,256]{4,3,2,1,0:T(8,128)(2,1)S(1)}, bf16[1,4,2,256,256]{4,3,2,1,0:T(8,128)(2,1)}, u32[]{:S(2)}) copy-start(bf16[1,4,2,256,256]{4,3,2,1,0:T(8,128)(2,1)} %param.5) | copy-start | bytes 3145732
  60.1 4.9 %copy-start.2 = (bf16[1,4,2,256,256]{4,3,2,1,0:T(8,128)(2,1)S(1)}, bf16[1,4,2,256,256]{4,3,2,1,0:T(8,128)(2,1)}, u32[]{:S(2)}) copy-start(bf16[1,4,2,256,256]{4,3,2,1,0:T(8,128)(2,1)} %param.7) | copy-start | bytes 3145732
  61.4 18.9 %all-to-all-start.1 = ((bf16[32,2,32,256]{3,2,1,0:T(8,128)(2,1)}), bf16[32,2,32,256]{3,2,1,0:T(8,128)(2,1)S(1)}, u32[]{:S(2)}, u32[]{:S(2)}) async-start(bf16[32,2,32,256]{3,2,1,0:T(8,128)(2,1)} %fusion.4), calls=%async_computation.1 | async-start | bytes 2097152 | tf_op jit(solution)/shard_map/all_to_all | solution.py:81
where the time goes:
time: 84.6 us; the launch traced here: 84.3 us
  waiting for transfers between devices  38.7 us (46%)
  blocking collectives  19 us (22%)
  matrix products  13.4 us (16%)
  local copies, waits for them, and re-layouts  5.79 us (7%)
  starting transfers between devices  4.85 us (6%)
  other arithmetic  2.23 us (3%)
    ppermute x1, waiting for transfers between devices, shifted(): lax.ppermute(value, axis, [(source, source + steps) for source in range(l...  23.5 us
    all_to_all x1, blocking collectives, shards(): lax.all_to_all(lesser, 'energy', split_axis=2, concat_axis=0, tiled=True)  19 us
    all_to_all x1, waiting for transfers between devices, shards(): lax.all_to_all(polar_rows, 'energy', split_axis=0, concat_axis=2, tiled=T...  15.2 us
    all_to_all x1, starting transfers between devices, shards(): lax.all_to_all(polar_rows, 'energy', split_axis=0, concat_axis=2, tiled=T...  3.56 us
    unnamed x15, local copies, waits for them, and re-layouts  3.45 us
  transfers between devices with their start and end apart: 2, of which 2 were waited for; matrix products, arithmetic and copies ran while one was open for 3% of the time, Pallas kernels for 0%

commit v1 on v0

--- a/solution.py
+++ b/solution.py
@@ -78,7 +78,12 @@
     ).astype(jnp.bfloat16)
     entries = lax.all_to_all(lesser, "energy", split_axis=2, concat_axis=0, tiled=True)
     polar_rows = correlate(entries)
-    back_field = lax.all_to_all(polar_rows, "energy", split_axis=0, concat_axis=2, tiled=True)
+    back_field = jnp.concatenate(
+        lax.all_to_all(
+            jnp.stack(jnp.split(polar_rows, lax.axis_size("energy"), axis=0)), "energy", 0, 0
+        ),
+        axis=2,
+    )
     screened_left = times_block(screening[0], back_field).astype(jnp.bfloat16)
     result_field = times_adjoint(screened_left, screening[0]).astype(jnp.bfloat16)
     return result_field[None]

time: 84.6 us -> 88.9 us (1.051)
  local copies, waits for them, and re-layouts: 5.79 us -> 11.1 us
  other arithmetic: 2.23 us -> 1.25 us
    unnamed x15 -> x22, local copies, waits for them, and re-layouts: 3.45 us -> 8.1 us
    convert_element_type x1, other arithmetic: 1.29 us -> 0.3 us  [correlate(): return polar.reshape(spread.shape).astype(jnp.bfloat16)]
where the time goes in v1:
time: 88.9 us; the launch traced here: 88.7 us
  waiting for transfers between devices  38.7 us (44%)
  blocking collectives  19 us (21%)
  matrix products  13.4 us (15%)
  local copies, waits for them, and re-layouts  11.1 us (12%)
  starting transfers between devices  4.85 us (5%)
  other arithmetic  1.25 us (1%)
    ppermute x1, waiting for transfers between devices, shifted(): lax.ppermute(value, axis, [(source, source + steps) for source in range(l...  23.5 us
    all_to_all x1, blocking collectives, shards(): lax.all_to_all(lesser, 'energy', split_axis=2, concat_axis=0, tiled=True)  19 us
    all_to_all x1, waiting for transfers between devices, shards(): lax.all_to_all(jnp.stack(jnp.split(polar_rows, lax.axis_size('energy'), a...  15.2 us
    unnamed x22, local copies, waits for them, and re-layouts  8.1 us
    all_to_all x1, starting transfers between devices, shards(): lax.all_to_all(jnp.stack(jnp.split(polar_rows, lax.axis_size('energy'), a...  3.56 us
  transfers between devices with their start and end apart: 2, of which 2 were waited for; matrix products, arithmetic and copies ran while one was open for 3% of the time, Pallas kernels for 0%

profile of v1, /device:TPU:0, one launch (start us, length us, event | category | flops | bytes accessed | tf_op | source)
XLA Modules:
  0.0 88.7 jit_solution(4998034310411438746)
XLA Ops:
  0.0 1.4 %copy.90 = bf16[1,4,2,256,256]{4,3,1,2,0:T(8,128)(2,1)S(1)} copy(bf16[1,4,2,256,256]{4,3,2,1,0:T(8,128)(2,1)} %param.6) | data formatting | bytes 2097152 | tf_op args[2]
  1.4 1.3 %collective-permute-start = (bf16[1,4,2,256,256]{4,3,1,2,0:T(8,128)(2,1)S(1)}, bf16[1,4,2,256,256]{4,3,1,2,0:T(8,128)(2,1)S(1)}, u32[]{:S(2)}, u32[]{:S(2)}) collective-permute-start(bf16[1,4,2,256,256]{4,3,1,2,0:T(8,128)(2,1)S(1)} %copy.90), channel_id=1, source_target_pairs={{1,0},{2,1},{3,2},{5,4},{6,5},{7,6},{9,8},{10,9},{11,10},{13,12},{... | collective-permute-start | bytes 3145736 | tf_op jit(solution)/shard_map/ppermute | solution.py:11
  4.0 0.6 copy-done.1
  6.0 23.5 %collective-permute-done = bf16[1,4,2,256,256]{4,3,1,2,0:T(8,128)(2,1)S(1)} collective-permute-done((bf16[1,4,2,256,256]{4,3,1,2,0:T(8,128)(2,1)S(1)}, bf16[1,4,2,256,256]{4,3,1,2,0:T(8,128)(2,1)S(1)}, u32[]{:S(2)}, u32[]{:S(2)}) %collective-permute-start) | collective-permute-done | bytes 1048608 | tf_op jit(solution)/shard_map/ppermute | solution.py:11
  32.1 0.4 fusion.3
  32.5 0.8 copy.58
  33.3 19.0 %all_to_all.23 = bf16[4,2,256,256]{3,0,1,2:T(4,128)(2,1)S(1)} all-to-all(bf16[4,2,256,256]{3,0,1,2:T(4,128)(2,1)S(1)} %copy.58), channel_id=1, replica_groups=mesh['energy'=8,'cuts'=4] {'energy'}, dimensions={2} | all-to-all | bytes 2097152 | tf_op jit(solution)/shard_map/all_to_all | solution.py:79
  53.4 0.8 fusion.59
  54.2 0.8 fusion.56
  55.0 0.8 convolution_add_fusion.1
  55.9 0.8 convolution_add_fusion
  57.1 1.2 %convolution_multiply_fusion.1 = f32[32,8192]{1,0:T(8,128)S(1)} fusion(f32[64,8192]{1,0:T(8,128)S(1)} %fusion.1), kind=kOutput, calls=%fused_computation.3 | convolution fusion | flops 201617408 | bytes 3145728 | tf_op jit(solution)/shard_map/dot_general | solution.py:66
  58.3 1.2 %convolution_multiply_fusion = f32[32,8192]{1,0:T(8,128)S(1)} fusion(f32[64,8192]{1,0:T(8,128)S(1)} %fusion.1), kind=kOutput, calls=%fused_computation.2 | convolution fusion | flops 201617408 | bytes 3145728 | tf_op jit(solution)/shard_map/dot_general | solution.py:67
  60.4 0.7 fusion.38
  61.1 0.7 fusion.37
  61.8 0.7 fusion.36
  62.4 0.7 fusion.35
  63.1 0.7 fusion.34
  63.8 0.7 fusion.33
  64.4 0.7 fusion.32
  65.1 0.7 fusion.31
  65.7 3.6 %all-to-all-start.1 = ((bf16[8,4,2,32,256]{4,3,2,1,0:T(8,128)(2,1)}), bf16[8,4,2,32,256]{4,3,2,1,0:T(8,128)(2,1)S(1)}, u32[]{:S(2)}, u32[]{:S(2)}) async-start(bf16[8,4,2,32,256]{4,3,2,1,0:T(8,128)(2,1)} %fusion.31), calls=%async_computation.1 | async-start | bytes 2097152 | tf_op jit(solution)/shard_map/all_to_all | solution.py:82
  69.4 15.2 %all-to-all-done.1 = bf16[8,4,2,32,256]{4,3,2,1,0:T(8,128)(2,1)S(1)} async-done(((bf16[8,4,2,32,256]{4,3,2,1,0:T(8,128)(2,1)}), bf16[8,4,2,32,256]{4,3,2,1,0:T(8,128)(2,1)S(1)}, u32[]{:S(2)}, u32[]{:S(2)}) %all-to-all-start.1) | async-done | bytes 1048608 | tf_op jit(solution)/shard_map/all_to_all | solution.py:82
  87.6 1.0 %copy.71 = bf16[1,4,2,256,256]{4,3,2,1,0:T(8,128)(2,1)} copy(bf16[1,4,2,256,256]{4,3,1,2,0:T(8,128)(2,1)S(1)} %pad_maximum_fusion) | data formatting | bytes 2097152 | tf_op jit(solution)/shard_map/stack | solution.py:31
  (45 shorter events, 10.6 us)
Async XLA Ops:
  0.0 2.7 %copy-start = (bf16[1,4,2,256,256]{4,3,2,1,0:T(8,128)(2,1)S(1)}, bf16[1,4,2,256,256]{4,3,2,1,0:T(8,128)(2,1)}, u32[]{:S(2)}) copy-start(bf16[1,4,2,256,256]{4,3,2,1,0:T(8,128)(2,1)} %param.4) | copy-start | bytes 3145732
  1.4 28.1 %collective-permute-start = (bf16[1,4,2,256,256]{4,3,1,2,0:T(8,128)(2,1)S(1)}, bf16[1,4,2,256,256]{4,3,1,2,0:T(8,128)(2,1)S(1)}, u32[]{:S(2)}, u32[]{:S(2)}) collective-permute-start(bf16[1,4,2,256,256]{4,3,1,2,0:T(8,128)(2,1)S(1)} %copy.90), channel_id=1, source_target_pairs={{1,0},{2,1},{3,2},{5,4},{6,5},{7,6},{9,8},{10,9},{11,10},{13,12},{... | collective-permute-start | bytes 3145736 | tf_op jit(solution)/shard_map/ppermute | solution.py:11
  3.4 1.2 %copy-start.1 = (bf16[1,4,2,256,256]{4,3,2,1,0:T(8,128)(2,1)S(1)}, bf16[1,4,2,256,256]{4,3,2,1,0:T(8,128)(2,1)}, u32[]{:S(2)}) copy-start(bf16[1,4,2,256,256]{4,3,2,1,0:T(8,128)(2,1)} %param.5) | copy-start | bytes 3145732
  60.4 8.9 %copy-start.2 = (bf16[1,4,2,256,256]{4,3,2,1,0:T(8,128)(2,1)S(1)}, bf16[1,4,2,256,256]{4,3,2,1,0:T(8,128)(2,1)}, u32[]{:S(2)}) copy-start(bf16[1,4,2,256,256]{4,3,2,1,0:T(8,128)(2,1)} %param.7) | copy-start | bytes 3145732
  65.7 18.9 %all-to-all-start.1 = ((bf16[8,4,2,32,256]{4,3,2,1,0:T(8,128)(2,1)}), bf16[8,4,2,32,256]{4,3,2,1,0:T(8,128)(2,1)S(1)}, u32[]{:S(2)}, u32[]{:S(2)}) async-start(bf16[8,4,2,32,256]{4,3,2,1,0:T(8,128)(2,1)} %fusion.31), calls=%async_computation.1 | async-start | bytes 2097152 | tf_op jit(solution)/shard_map/all_to_all | solution.py:82
